TPU v7x, 512 devices: a whole 4x4x16 slice. The times are simulated.
512 devices in a mesh: grp: 32 (over y, x, core), tp: 16 (over z).
Axes of the slice: x: 4, y: 4, z: 16, core: 2. Of those that a mesh axis runs over, the one named last changes fastest.
Arguments:
- trainer_increment: float32 [1024, 128, 128], P(('tp', 'grp')), may hold values from -0.3125 to 0.3125
- trainer_residual: float32 [1024, 128, 128], P(('tp', 'grp')), may hold values from -0.3125 to 0.3125
- partition_tile_indices: int32 [512, 2], P(('tp', 'grp')), may hold values from 0 to 1, as said below
- retained_tallies: int32 [512], P(('tp', 'grp')), may hold values from 0 to 2, as said below
- projection_parameters: bfloat16 [8192, 2048], P('tp'), may hold values from -0.0625 to 0.0625
- normalized_activations: bfloat16 [4, 32, 8192], P(None, 'grp', 'tp'), may hold values from -6 to 6
- rotated_questions: bfloat16 [4, 32, 8192], P(None, 'grp'), may hold values from -256 to 256
- stored_attention_memory: bfloat16 [32, 8192, 2048], P('grp', 'tp'), may hold values from -6 to 6
- memory_fill_lengths: int32 [32], P('grp'), may hold values from 2 to 8192, as said below
Outputs:
- new_error: float32 [1024, 128, 128], P(('tp', 'grp'))
- new_kv: bfloat16 [4, 32, 2048], P(None, 'grp', 'tp')
- attention: bfloat16 [4, 32, 8192], P(None, 'grp', 'tp')
Inputs may be any that keep to these rules, and one draw needn't show every extreme that they name: `partition_tile_indices`: each row lists the local block numbers of one shard, each once; only its first retained_tallies entries name surviving blocks. `retained_tallies`: some shard lists all 2 of its blocks in every draw. Row r's valid cache positions are 0 to memory_fill_lengths[r] - 1; some row has all 8192 in every draw.
All inputs are finite; a program needn't handle non-finite values.
Results may differ from a plain program's by a relative error of at most 0.02.
Values may be sent and summed in bfloat16 or wider, within the bound.
A program may use at most 64 MiB of HBM per device.

v0:
```python
import math
import jax
import jax.numpy as jnp
from jax import lax
from jax.sharding import PartitionSpec as P

HD = 128
BLK = 128
NEG = -1e30


def merged(array, axis, combine):
    everything = jax.tree.map(lambda part: lax.all_gather(part, axis), array)
    initial = jax.tree.map(lambda part: part[0], everything)

    def step(k, so_far):
        return combine(so_far, jax.tree.map(lambda part: part[k], everything))

    return lax.fori_loop(1, lax.axis_size(axis), step, initial)


def retained_tiles(partition_tile_indices, retained_tallies):
    slots = partition_tile_indices.shape[1]
    sorting_permutation = jnp.arange(slots, dtype=jnp.int32)
    enumerated_tiles = sorting_permutation[None, :] < retained_tallies[:, None]
    hits = (
        partition_tile_indices[:, :, None] == sorting_permutation[None, None, :]
    ) & enumerated_tiles[:, :, None]
    return jnp.any(hits, axis=1)


def combine(first, second):
    top_a, total_a, blended_first = first
    top_b, total_b, mixed_b = second
    top = jnp.maximum(top_a, top_b)
    scale_a = jnp.exp(top_a - top)
    scale_b = jnp.exp(top_b - top)
    total = total_a * scale_a + total_b * scale_b
    mixed = blended_first * scale_a[..., None] + mixed_b * scale_b[..., None]
    return (top, total, mixed)


def cache_partial(rotated_questions, stored_attention_memory, memory_fill_lengths, first):
    steps, rows, width = rotated_questions.shape
    span = stored_attention_memory.shape[1]
    heads_kv = stored_attention_memory.shape[2] // (2 * HD)
    group = width // HD // heads_kv
    scale = 1.0 / math.sqrt(HD)
    query = rotated_questions.reshape(steps, rows, heads_kv, group, HD)
    cache_rows_held = stored_attention_memory.reshape(rows, span, heads_kv, 2, HD)
    scores = (
        jnp.einsum(
            "srhgd,rphd->srhgp",
            query,
            cache_rows_held[:, :, :, 0],
            preferred_element_type=jnp.float32,
        )
        * scale
    )
    position = first + jnp.arange(span, dtype=jnp.int32)
    valid = (position[None, :] < memory_fill_lengths[:, None])[None, :, None, None, :]
    scores = jnp.where(valid, scores, NEG)
    top = jnp.max(scores, axis=-1)
    probs = jnp.where(valid, jnp.exp(scores - top[..., None]), 0.0)
    total = jnp.sum(probs, axis=-1)
    values = cache_rows_held[:, :, :, 1].astype(jnp.float32)
    mixed = jnp.einsum("srhgp,rphd->srhgd", probs, values, precision=lax.Precision.HIGHEST)
    heads = heads_kv * group
    return (
        top.reshape(steps, rows, heads),
        total.reshape(steps, rows, heads),
        mixed.reshape(steps, rows, heads, HD),
    )


def body(
    trainer_increment,
    trainer_residual,
    partition_tile_indices,
    retained_tallies,
    projection_parameters,
    normalized_activations,
    rotated_questions,
    stored_attention_memory,
    memory_fill_lengths,
):
    summed = trainer_increment + trainer_residual
    retain_markers = retained_tiles(partition_tile_indices, retained_tallies).reshape(-1)
    sent = jnp.where(
        retain_markers[:, None, None], summed.astype(jnp.bfloat16), jnp.zeros((), jnp.bfloat16)
    )
    new_error = summed - sent.astype(jnp.float32)
    blocks = lax.all_gather(sent, "grp", axis=0, tiled=True)
    local_feats, kvw = projection_parameters.shape
    update = (
        blocks.reshape(local_feats // BLK, kvw // BLK, BLK, BLK)
        .transpose(0, 2, 1, 3)
        .reshape(local_feats, kvw)
    )
    patched = (projection_parameters.astype(jnp.float32) + update.astype(jnp.float32)).astype(
        jnp.bfloat16
    )
    steps, local_rows, width = normalized_activations.shape
    partial_kv = jnp.dot(
        normalized_activations.reshape(steps * local_rows, width),
        patched,
        preferred_element_type=jnp.float32,
    )
    ranks = lax.axis_size("tp")
    rank = lax.axis_index("tp")
    columns = kvw // ranks
    kv_full = lax.psum(partial_kv, "tp").astype(jnp.bfloat16)
    kv_own = lax.dynamic_slice_in_dim(kv_full, rank * columns, columns, 1)
    new_kv = kv_own.reshape(steps, local_rows, columns)
    span = stored_attention_memory.shape[1]
    top, total, mixed = cache_partial(
        rotated_questions, stored_attention_memory, memory_fill_lengths, rank * span
    )
    heads = top.shape[2]
    own = heads // ranks
    top, total, mixed = merged((top, total, mixed), "tp", combine)
    top = lax.dynamic_slice_in_dim(top, rank * own, own, 2)
    total = lax.dynamic_slice_in_dim(total, rank * own, own, 2)
    mixed = lax.dynamic_slice_in_dim(mixed, rank * own, own, 2)
    heads_kv = kvw // (2 * HD)
    group = heads // heads_kv
    scale = 1.0 / math.sqrt(HD)
    fresh = kv_full.reshape(steps, local_rows, heads_kv, 2, HD)
    head_ids = (rank * own + jnp.arange(own, dtype=jnp.int32)) // group
    fresh = jnp.take(fresh, head_ids, axis=2)
    query = lax.dynamic_slice_in_dim(rotated_questions, rank * own * HD, own * HD, 2).reshape(
        steps, local_rows, own, HD
    )
    scores = (
        jnp.einsum("srjd,urjd->srju", query, fresh[:, :, :, 0], preferred_element_type=jnp.float32)
        * scale
    )
    step_ids = jnp.arange(steps, dtype=jnp.int32)
    causal = (step_ids[None, :] <= step_ids[:, None])[:, None, None, :]
    scores = jnp.where(causal, scores, NEG)
    peak = jnp.maximum(top, jnp.max(scores, axis=-1))
    probs = jnp.where(causal, jnp.exp(scores - peak[..., None]), 0.0)
    carried = jnp.exp(top - peak)
    denom = total * carried + jnp.sum(probs, axis=-1)
    values = fresh[:, :, :, 1].astype(jnp.float32)
    numer = mixed * carried[..., None] + jnp.einsum(
        "srju,urjd->srjd", probs, values, precision=lax.Precision.HIGHEST
    )
    attention = (numer / denom[..., None]).reshape(steps, local_rows, own * HD).astype(jnp.bfloat16)
    return (new_error, new_kv, attention)


def solution(mesh):
    placed = (
        P(("tp", "grp"), None, None),
        P(("tp", "grp"), None, None),
        P(("tp", "grp"), None),
        P(("tp", "grp")),
        P("tp", None),
        P(None, "grp", "tp"),
        P(None, "grp", None),
        P("grp", "tp", None),
        P("grp"),
    )
    return jax.shard_map(
        body,
        mesh=mesh,
        in_specs=placed,
        out_specs=(P(("tp", "grp"), None, None), P(None, "grp", "tp"), P(None, "grp", "tp")),
        check_vma=False,
    )
```

profile of v0, /device:TPU:2, one launch (start us, length us, event | category | flops | bytes accessed | tf_op | source)
XLA Modules:
  0.0 221.9 jit_solution(10214104289567611357)
XLA Ops:
  7.2 0.0 copy-start
  7.2 0.0 all-gather.5.cloned.1.call-start
  7.2 0.0 copy-start.4
  7.2 2.9 %copy.91 = bf16[1,512,2048]{1,2,0:T(8,128)(2,1)S(1)} copy(bf16[1,512,2048]{2,1,0:T(8,128)(2,1)} %param.18) | data formatting | bytes 4194304 | tf_op args[7]
  10.8 0.0 copy-done.4
  10.8 0.0 copy-start.5
  10.8 0.0 copy-start.2
  10.8 0.0 copy-start.3
  10.9 0.4 fusion.34
  11.2 1.1 convolution_bitcast_fusion.1
  12.4 0.7 copy.134
  13.0 0.0 all-gather.5.cloned.1.call-update
  13.1 0.0 all-gather.3.cloned.1.call-start
  13.8 0.0 copy-done.5
  13.8 0.1 and_reduce_fusion
  13.9 0.0 copy-done.2
  13.9 0.0 copy-done.3
  13.9 0.7 convert_select_fusion
  14.6 0.0 all-gather.3.cloned.1.call-update
  14.6 0.7 convert_subtract_fusion
  15.3 0.2 fusion.13
  15.6 0.1 all_gather_reshape.9
  15.7 35.6 %all_gather.13 = f32[16,4,1,64]{3,1,2,0:T(4,128)S(1)} all-gather(f32[1,4,1,64]{3,1,2,0:T(4,128)S(1)} %all_gather_reshape.9), channel_id=1, replica_groups=mesh['grp'=32,'tp'=16] {'tp'}, dimensions={0}, use_global_device_ids=true | all-gather | bytes 17408 | tf_op jit(solution)/shard_map/all_gather | solution.py:13
  51.3 0.1 all_gather_reshape.10
  51.4 26.1 %all_gather.14 = f32[16,4,1,64]{3,1,2,0:T(4,128)S(1)} all-gather(f32[1,4,1,64]{3,1,2,0:T(4,128)S(1)} %all_gather_reshape.10), channel_id=1, replica_groups=mesh['grp'=32,'tp'=16] {'tp'}, dimensions={0}, use_global_device_ids=true | all-gather | bytes 17408 | tf_op jit(solution)/shard_map/all_gather | solution.py:13
  77.5 13.1 %all-gather.5.cloned.1.call-done = f32[16,4,1,64,128]{4,3,2,1,0:T(8,128)} async-done(((f32[1,4,1,64,128]{4,3,2,1,0:T(8,128)}), f32[16,4,1,64,128]{4,3,2,1,0:T(8,128)}) %all-gather.5.cloned.1.call-update) | async-done | bytes 2097168 | tf_op jit(solution)/shard_map/all_gather | solution.py:13
  90.5 0.9 slice_bitcast_fusion.4
  91.5 17.1 %while.19 = (s32[]{:T(128)}, f32[4,1,64]{2,1,0:T(1,128)S(1)}, f32[4,1,64]{2,1,0:T(1,128)S(1)}, f32[4,1,64,128]{3,2,1,0:T(8,128)S(1)}, f32[16,4,1,64]{3,1,2,0:T(4...) while((s32[]{:T(128)}, f32[4,1,64]{2,1,0:T(1,128)S(1)}, ...), condition=%wide.region_5.6_spmd, body=%wide.region_4.5_spmd.sunk | while | flops 99845 | bytes 407703 | solution.py:19
  91.5 1.1 fusion.37
  92.7 1.1 fusion.37
  93.8 1.1 fusion.37
  94.9 1.1 fusion.37
  96.1 1.1 fusion.37
  97.2 1.1 fusion.37
  98.4 1.1 fusion.37
  99.5 1.1 fusion.37
  100.6 1.1 fusion.37
  101.8 1.1 fusion.37
  102.9 1.1 fusion.37
  104.1 1.1 fusion.37
  105.2 1.1 fusion.37
  106.3 1.1 fusion.37
  107.5 1.1 fusion.37
  108.6 0.1 copy.103
  108.7 40.8 %all-gather.3.cloned.1.call-done = bf16[64,128,128]{2,1,0:T(8,128)(2,1)} async-done(((bf16[2,128,128]{2,1,0:T(8,128)(2,1)}), bf16[64,128,128]{2,1,0:T(8,128)(2,1)}) %all-gather.3.cloned.1.call-update) | async-done | bytes 2097168 | tf_op jit(solution)/shard_map/all_gather | solution.py:93
  149.5 2.1 convert_bitcast_fusion
  151.6 0.0 copy-start.1
  151.6 2.4 %copy.90 = f32[4,128,16,128]{3,2,1,0:T(8,128)S(1)} copy(f32[4,128,16,128]{3,1,2,0:T(8,128)S(1)} %convert_bitcast_fusion) | data formatting | bytes 8388608 | tf_op jit(solution)/shard_map/convert_element_type | solution.py:100
  154.0 0.0 copy-done
  154.0 0.0 copy-done.1
  154.1 1.3 convolution_bitcast_fusion
  155.4 56.9 %psum.7 = bf16[4,2048]{1,0:T(4,128)(2,1)S(1)} all-reduce(f32[4,2048]{1,0:T(4,128)S(1)} %convolution_bitcast_fusion), channel_id=1, replica_groups=mesh['grp'=32,'tp'=16] {'tp'}, use_global_device_ids=true, to_apply=%region_1.2 | all-reduce | flops 8192 | bytes 49152 | tf_op jit(solution)/shard_map/psum | solution.py:112
  212.3 0.6 fusion.29
  212.8 0.6 gather_fusion
  213.4 0.1 bitcast_select_fusion
  213.5 0.1 fusion.35
  213.6 0.1 copy.107
  213.7 0.1 fusion.27
  213.8 0.1 copy.109
  213.9 0.1 copy.113
  214.0 0.1 fusion.31
  214.1 0.1 copy.114
  214.2 0.1 copy.108
  214.3 0.8 fusion.10
  (41 shorter events, 0.6 us)
Async XLA Ops:
  7.2 146.9 %copy-start = (bf16[4,1,512]{2,0,1:T(4,128)(2,1)S(1)}, bf16[4,1,512]{2,0,1:T(4,128)(2,1)}, u32[]{:S(2)}) copy-start(bf16[4,1,512]{2,0,1:T(4,128)(2,1)} %param.16) | copy-start | bytes 12292
  7.2 83.4 %all-gather.5.cloned.1.call-start = ((), (), s32[]{:S(2)}) async-start(), calls=%async_computation.1 | async-start | bytes 2228224 | tf_op jit(solution)/shard_map/all_gather | solution.py:13
  7.2 3.6 %copy-start.4 = (bf16[4,1,8192]{2,0,1:T(4,128)(2,1)S(1)}, bf16[4,1,8192]{2,0,1:T(4,128)(2,1)}, u32[]{:S(2)}) copy-start(bf16[4,1,8192]{2,0,1:T(4,128)(2,1)} %param.17) | copy-start | bytes 196612
  10.8 3.0 %copy-start.5 = (s32[1,2]{1,0:T(1,128)S(1)}, s32[1,2]{1,0:T(1,128)}, u32[]{:S(2)}) copy-start(s32[1,2]{1,0:T(1,128)} %param.13) | copy-start | bytes 28
  10.8 3.0 %copy-start.2 = (f32[2,128,128]{2,1,0:T(8,128)S(1)}, f32[2,128,128]{2,1,0:T(8,128)}, u32[]{:S(2)}) copy-start(f32[2,128,128]{2,1,0:T(8,128)} %param.11) | copy-start | bytes 393220
  10.8 3.0 %copy-start.3 = (f32[2,128,128]{2,1,0:T(8,128)S(1)}, f32[2,128,128]{2,1,0:T(8,128)}, u32[]{:S(2)}) copy-start(f32[2,128,128]{2,1,0:T(8,128)} %param.12) | copy-start | bytes 393220
  13.1 136.4 %all-gather.3.cloned.1.call-start = ((), (), s32[]{:S(2)}) async-start(), calls=%async_computation | async-start | bytes 2162688 | tf_op jit(solution)/shard_map/all_gather | solution.py:93
  151.6 2.5 %copy-start.1 = (bf16[512,2048]{1,0:T(8,128)(2,1)S(1)}, bf16[512,2048]{1,0:T(8,128)(2,1)}, u32[]{:S(2)}) copy-start(bf16[512,2048]{1,0:T(8,128)(2,1)} %param.15) | copy-start | bytes 6291460
Sparse Core Ops, SparseCore 0:
  13.2 77.3 all-gather.4
  93.7 55.7 all-gather.2
where the time goes:
time: 222 us
  blocking collectives  119 us (54%)
  waiting for transfers between devices  53.9 us (24%)
  other arithmetic  20.7 us (9%)
  between operations  15.5 us (7%)
  local copies, waits for them, and re-layouts  8.93 us (4%)
  matrix products  3.81 us (2%)
    all_gather x2, blocking collectives, merged(): everything = jax.tree.map(lambda part: lax.all_gather(part, axis), array)  61.6 us
    psum x1, blocking collectives, body(): kv_full = lax.psum(partial_kv, 'tp').astype(jnp.bfloat16)  56.9 us
    all_gather x1, waiting for transfers between devices, body(): blocks = lax.all_gather(sent, 'grp', axis=0, tiled=True)  40.8 us
    add x15, other arithmetic, combine(): mixed = blended_first * scale_a[..., None] + mixed_b * scale_b[..., None]  16.1 us
    all_gather x1, waiting for transfers between devices, merged(): everything = jax.tree.map(lambda part: lax.all_gather(part, axis), array)  13.1 us
  transfers between devices with their start and end apart: 2, of which 2 were waited for; matrix products, arithmetic and copies ran while one was open for 9% of the time, Pallas kernels for 0%

commit v1 on v0

--- a/solution.py
+++ b/solution.py
@@ -109,7 +109,7 @@
     ranks = lax.axis_size("tp")
     rank = lax.axis_index("tp")
     columns = kvw // ranks
-    kv_full = lax.psum(partial_kv, "tp").astype(jnp.bfloat16)
+    kv_full = jnp.sum(lax.all_gather(partial_kv, "tp"), axis=0).astype(jnp.bfloat16)
     kv_own = lax.dynamic_slice_in_dim(kv_full, rank * columns, columns, 1)
     new_kv = kv_own.reshape(steps, local_rows, columns)
     span = stored_attention_memory.shape[1]

time: 222 us -> 199 us (0.90)
  blocking collectives: 119 us -> 95.1 us
    psum x1 -> x0, blocking collectives: 56.9 us -> none  [body(): kv_full = lax.psum(partial_kv, 'tp').astype(jnp.bfloat16)]
    all_gather x0 -> x1, blocking collectives: none -> 33.5 us  [body(): lax.all_gather(partial_kv, 'tp')]
  transfers between devices with their start and end apart: 2 -> 2, of which waited for: 2 -> 2; matrix products, arithmetic and copies ran while one was open for 9% -> 10% of each run, Pallas kernels for 0% -> 0%
where the time goes in v1:
time: 199 us
  blocking collectives  95.1 us (48%)
  waiting for transfers between devices  53.9 us (27%)
  other arithmetic  20.8 us (10%)
  between operations  15.5 us (8%)
  local copies, waits for them, and re-layouts  8.94 us (4%)
  matrix products  3.81 us (2%)
    all_gather x2, blocking collectives, merged(): everything = jax.tree.map(lambda part: lax.all_gather(part, axis), array)  61.6 us
    all_gather x1, waiting for transfers between devices, body(): blocks = lax.all_gather(sent, 'grp', axis=0, tiled=True)  40.8 us
    all_gather x1, blocking collectives, body(): lax.all_gather(partial_kv, 'tp')  33.5 us
    add x15, other arithmetic, combine(): mixed = blended_first * scale_a[..., None] + mixed_b * scale_b[..., None]  16.1 us
    all_gather x1, waiting for transfers between devices, merged(): everything = jax.tree.map(lambda part: lax.all_gather(part, axis), array)  13.1 us
  transfers between devices with their start and end apart: 2, of which 2 were waited for; matrix products, arithmetic and copies ran while one was open for 10% of the time, Pallas kernels for 0%

profile of v1, /device:TPU:2, one launch (start us, length us, event | category | flops | bytes accessed | tf_op | source)
XLA Modules:
  0.0 198.7 jit_solution(14276287727001649753)
XLA Ops:
  7.2 0.0 copy-start
  7.2 0.0 all-gather.7.cloned.1.call-start
  7.2 0.0 copy-start.4
  7.2 2.9 %copy.88 = bf16[1,512,2048]{1,2,0:T(8,128)(2,1)S(1)} copy(bf16[1,512,2048]{2,1,0:T(8,128)(2,1)} %param.18) | data formatting | bytes 4194304 | tf_op args[7]
  10.8 0.0 copy-done.4
  10.8 0.0 copy-start.5
  10.8 0.0 copy-start.2
  10.8 0.0 copy-start.3
  10.9 0.4 fusion.34
  11.2 1.1 convolution_bitcast_fusion.1
  12.4 0.7 copy.130
  13.0 0.0 all-gather.7.cloned.1.call-update
  13.1 0.0 all-gather.5.cloned.1.call-start
  13.8 0.0 copy-done.5
  13.8 0.1 and_reduce_fusion
  13.9 0.0 copy-done.2
  13.9 0.0 copy-done.3
  13.9 0.7 convert_select_fusion
  14.6 0.0 all-gather.5.cloned.1.call-update
  14.6 0.7 convert_subtract_fusion
  15.3 0.2 fusion.13
  15.6 0.1 all_gather_reshape.9
  15.7 35.6 %all_gather.21 = f32[16,4,1,64]{3,1,2,0:T(4,128)S(1)} all-gather(f32[1,4,1,64]{3,1,2,0:T(4,128)S(1)} %all_gather_reshape.9), channel_id=1, replica_groups=mesh['grp'=32,'tp'=16] {'tp'}, dimensions={0}, use_global_device_ids=true | all-gather | bytes 17408 | tf_op jit(solution)/shard_map/all_gather | solution.py:13
  51.3 0.1 all_gather_reshape.10
  51.4 26.1 %all_gather.22 = f32[16,4,1,64]{3,1,2,0:T(4,128)S(1)} all-gather(f32[1,4,1,64]{3,1,2,0:T(4,128)S(1)} %all_gather_reshape.10), channel_id=1, replica_groups=mesh['grp'=32,'tp'=16] {'tp'}, dimensions={0}, use_global_device_ids=true | all-gather | bytes 17408 | tf_op jit(solution)/shard_map/all_gather | solution.py:13
  77.5 13.1 %all-gather.7.cloned.1.call-done = f32[16,4,1,64,128]{4,3,2,1,0:T(8,128)} async-done(((f32[1,4,1,64,128]{4,3,2,1,0:T(8,128)}), f32[16,4,1,64,128]{4,3,2,1,0:T(8,128)}) %all-gather.7.cloned.1.call-update) | async-done | bytes 2097168 | tf_op jit(solution)/shard_map/all_gather | solution.py:13
  90.5 0.9 slice_bitcast_fusion.4
  91.5 17.1 %while.19 = (s32[]{:T(128)}, f32[4,1,64]{2,1,0:T(1,128)S(1)}, f32[4,1,64]{2,1,0:T(1,128)S(1)}, f32[4,1,64,128]{3,2,1,0:T(8,128)S(1)}, f32[16,4,1,64]{3,1,2,0:T(4...) while((s32[]{:T(128)}, f32[4,1,64]{2,1,0:T(1,128)S(1)}, ...), condition=%wide.region_5.6_spmd, body=%wide.region_4.5_spmd.sunk | while | flops 99845 | bytes 407703 | solution.py:19
  91.5 1.1 fusion.37
  92.7 1.1 fusion.37
  93.8 1.1 fusion.37
  94.9 1.1 fusion.37
  96.1 1.1 fusion.37
  97.2 1.1 fusion.37
  98.4 1.1 fusion.37
  99.5 1.1 fusion.37
  100.6 1.1 fusion.37
  101.8 1.1 fusion.37
  102.9 1.1 fusion.37
  104.1 1.1 fusion.37
  105.2 1.1 fusion.37
  106.3 1.1 fusion.37
  107.5 1.1 fusion.37
  108.6 0.1 copy.100
  108.7 40.8 %all-gather.5.cloned.1.call-done = bf16[64,128,128]{2,1,0:T(8,128)(2,1)} async-done(((bf16[2,128,128]{2,1,0:T(8,128)(2,1)}), bf16[64,128,128]{2,1,0:T(8,128)(2,1)}) %all-gather.5.cloned.1.call-update) | async-done | bytes 2097168 | tf_op jit(solution)/shard_map/all_gather | solution.py:93
  149.5 2.1 %convert_bitcast_fusion = f32[4,128,16,128]{3,1,2,0:T(8,128)S(1)} fusion(bf16[4,16,128,128]{3,2,1,0:T(8,128)(2,1)} %bitcast.169), kind=kLoop, calls=%fused_computation.10 | loop fusion | flops 1048576 | bytes 6291456 | tf_op jit(solution)/shard_map/convert_element_type | solution.py:100
  151.6 0.0 copy-start.1
  151.6 2.4 %copy.87 = f32[4,128,16,128]{3,2,1,0:T(8,128)S(1)} copy(f32[4,128,16,128]{3,1,2,0:T(8,128)S(1)} %convert_bitcast_fusion) | data formatting | bytes 8388608 | tf_op jit(solution)/shard_map/convert_element_type | solution.py:100
  154.0 0.0 copy-done
  154.1 1.3 convolution_bitcast_fusion
  155.4 33.5 %all-gather.1 = f32[16,4,2048]{2,1,0:T(4,128)S(1)} all-gather(f32[1,4,2048]{2,1,0:T(4,128)S(1)} %convolution_bitcast_fusion), channel_id=2, replica_groups=mesh['grp'=32,'tp'=16] {'tp'}, dimensions={0}, use_global_device_ids=true | all-gather | bytes 557056 | tf_op jit(solution)/shard_map/all_gather | solution.py:112
  188.9 0.1 reduce_sum.29
  189.0 0.6 fusion.29
  189.5 0.6 gather_fusion
  190.1 0.1 bitcast_select_fusion
  190.2 0.1 fusion.35
  190.3 0.1 copy.103
  190.4 0.1 fusion.27
  190.5 0.1 copy.105
  190.6 0.1 copy.109
  190.7 0.1 fusion.31
  190.8 0.1 copy.110
  190.9 0.1 copy.104
  191.0 0.8 fusion.10
  (42 shorter events, 0.6 us)
Async XLA Ops:
  7.2 146.9 %copy-start = (bf16[4,1,512]{2,0,1:T(4,128)(2,1)S(1)}, bf16[4,1,512]{2,0,1:T(4,128)(2,1)}, u32[]{:S(2)}) copy-start(bf16[4,1,512]{2,0,1:T(4,128)(2,1)} %param.16) | copy-start | bytes 12292
  7.2 83.4 %all-gather.7.cloned.1.call-start = ((), (), s32[]{:S(2)}) async-start(), calls=%async_computation.1 | async-start | bytes 2228224 | tf_op jit(solution)/shard_map/all_gather | solution.py:13
  7.2 3.6 %copy-start.4 = (bf16[4,1,8192]{2,0,1:T(4,128)(2,1)S(1)}, bf16[4,1,8192]{2,0,1:T(4,128)(2,1)}, u32[]{:S(2)}) copy-start(bf16[4,1,8192]{2,0,1:T(4,128)(2,1)} %param.17) | copy-start | bytes 196612
  10.8 3.0 %copy-start.5 = (s32[1,2]{1,0:T(1,128)S(1)}, s32[1,2]{1,0:T(1,128)}, u32[]{:S(2)}) copy-start(s32[1,2]{1,0:T(1,128)} %param.13) | copy-start | bytes 28
  10.8 3.0 %copy-start.2 = (f32[2,128,128]{2,1,0:T(8,128)S(1)}, f32[2,128,128]{2,1,0:T(8,128)}, u32[]{:S(2)}) copy-start(f32[2,128,128]{2,1,0:T(8,128)} %param.11) | copy-start | bytes 393220
  10.8 3.0 %copy-start.3 = (f32[2,128,128]{2,1,0:T(8,128)S(1)}, f32[2,128,128]{2,1,0:T(8,128)}, u32[]{:S(2)}) copy-start(f32[2,128,128]{2,1,0:T(8,128)} %param.12) | copy-start | bytes 393220
  13.1 136.4 %all-gather.5.cloned.1.call-start = ((), (), s32[]{:S(2)}) async-start(), calls=%async_computation | async-start | bytes 2162688 | tf_op jit(solution)/shard_map/all_gather | solution.py:93
  151.6 2.5 %copy-start.1 = (bf16[512,2048]{1,0:T(8,128)(2,1)S(1)}, bf16[512,2048]{1,0:T(8,128)(2,1)}, u32[]{:S(2)}) copy-start(bf16[512,2048]{1,0:T(8,128)(2,1)} %param.15) | copy-start | bytes 6291460
Sparse Core Ops, SparseCore 0:
  13.2 77.3 all-gather.6
  93.7 55.7 all-gather.4
